TPU v7x, 512 devices: a whole 4x8x8 slice. The times are simulated.
512 devices in a mesh: seq: 16 (over z, core), ctx: 32 (over y, x).
Axes of the slice: x: 4, y: 8, z: 8, core: 2. Of those that a mesh axis runs over, the one named last changes fastest.
Arguments:
- queries: bfloat16 [65536, 2048], P(('seq', 'ctx')), parts along dimension 0, may hold values from -6 to 6
- key_rows: bfloat16 [65536, 2048], P(('seq', 'ctx')), parts along dimension 0, may hold values from -6 to 6
- values: bfloat16 [65536, 2048], P(('seq', 'ctx')), parts along dimension 0, may hold values from -6 to 6
- out_grad: bfloat16 [65536, 2048], P(('seq', 'ctx')), parts along dimension 0, may hold values from -0.008239746 to 0.008239746
- feature_map: bfloat16 [16, 128, 128], replicated, may hold values from -0.5 to 0.5
Outputs:
- query_grad: bfloat16 [65536, 2048], P(('seq', 'ctx')), parts along dimension 0
- key_grad: bfloat16 [65536, 2048], P(('seq', 'ctx')), parts along dimension 0
- value_grad: bfloat16 [65536, 2048], P(('seq', 'ctx')), parts along dimension 0
- map_grad: float32 [256, 128, 128], P('seq'), parts along dimension 0
There are 16 independent parts, one for each index of `seq`. A program takes and returns all parts, laid end to end along the dimension named above; an argument that names none is the same for every part. Nothing has to cross between parts.
All inputs are finite; a program needn't handle non-finite values.
Results may differ from a plain program's by a relative error of at most 0.033.
Values may be sent and summed in bfloat16 or wider, within the bound.
A program may use at most 128 MiB of HBM per device.

v0:
```python
import math

import jax
import jax.numpy as jnp
from jax import lax
from jax.sharding import PartitionSpec as P


def carried_in(part, axis, combine, identity, reverse):
    count = lax.axis_size(axis)
    place = lax.axis_index(axis)
    ahead = count - 1 - place if reverse else place
    gathered = lax.all_gather(part, axis)
    state = jnp.zeros_like(part) + jnp.asarray(identity, part.dtype)

    def one(turn, state):
        source = count - 1 - turn if reverse else turn
        return combine(state, lax.dynamic_index_in_dim(gathered, source, 0, False))

    return lax.fori_loop(0, ahead, one, state)


def add_states(earlier, later):
    return earlier + later


def per_device(queries, key_rows, values, out_grad, feature_map):
    f32 = jnp.float32
    bf16 = jnp.bfloat16
    length_dev = queries.shape[0]
    heads_count = feature_map.shape[0]
    head_size = feature_map.shape[1]
    shape_heads = (length_dev, heads_count, head_size)
    query_h = queries.reshape(shape_heads)
    key_h = key_rows.reshape(shape_heads)
    value_h = values.reshape(shape_heads)
    grad_h = out_grad.reshape(shape_heads)
    query_feat = jnp.einsum(
        "thd,hde->the", query_h, feature_map, preferred_element_type=f32
    ).astype(bf16)
    key_feat = jnp.einsum("thd,hde->the", key_h, feature_map, preferred_element_type=f32).astype(
        bf16
    )
    key_state = jnp.einsum("the,thv->hev", key_feat, value_h, preferred_element_type=f32).astype(
        bf16
    )
    grad_state = jnp.einsum("the,thv->hev", query_feat, grad_h, preferred_element_type=f32).astype(
        bf16
    )
    zeros_state = jnp.zeros_like(key_state)
    prefix = carried_in(key_state, "ctx", add_states, zeros_state, False).astype(f32)
    suffix = carried_in(grad_state, "ctx", add_states, zeros_state, True).astype(f32)
    prefix = prefix.astype(bf16)
    suffix = suffix.astype(bf16)
    rows_idx = lax.broadcasted_iota(jnp.int32, (length_dev, length_dev), 0)
    cols_idx = lax.broadcasted_iota(jnp.int32, (length_dev, length_dev), 1)
    causal = rows_idx >= cols_idx
    scores = jnp.einsum("the,she->hts", query_feat, key_feat, preferred_element_type=f32)
    scores = jnp.where(causal, scores, 0.0).astype(bf16)
    mixing = jnp.einsum("thv,shv->hts", grad_h, value_h, preferred_element_type=f32)
    mixing = jnp.where(causal, mixing, 0.0).astype(bf16)
    feat_qgrad = (
        jnp.einsum("hts,she->the", mixing, key_feat, preferred_element_type=f32)
        + jnp.einsum("thv,hev->the", grad_h, prefix, preferred_element_type=f32)
    ).astype(bf16)
    feat_kgrad = (
        jnp.einsum("hts,the->she", mixing, query_feat, preferred_element_type=f32)
        + jnp.einsum("shv,hev->she", value_h, suffix, preferred_element_type=f32)
    ).astype(bf16)
    value_grad = jnp.einsum(
        "hts,thv->shv", scores, grad_h, preferred_element_type=f32
    ) + jnp.einsum("she,hev->shv", key_feat, suffix, preferred_element_type=f32)
    query_grad = jnp.einsum("the,hde->thd", feat_qgrad, feature_map, preferred_element_type=f32)
    key_grad = jnp.einsum("the,hde->thd", feat_kgrad, feature_map, preferred_element_type=f32)
    local_grad = jnp.einsum(
        "thd,the->hde", query_h, feat_qgrad, preferred_element_type=f32
    ) + jnp.einsum("thd,the->hde", key_h, feat_kgrad, preferred_element_type=f32)
    local_grad = local_grad.astype(bf16).astype(f32)
    map_grad = lax.psum(local_grad.astype(jnp.bfloat16), "ctx").astype(jnp.float32) / math.sqrt(
        length_dev * lax.axis_size("ctx")
    )
    flat_shape = (length_dev, heads_count * head_size)
    return (
        query_grad.reshape(flat_shape).astype(bf16),
        key_grad.reshape(flat_shape).astype(bf16),
        value_grad.reshape(flat_shape).astype(bf16),
        map_grad,
    )


def solution(mesh):
    placed = (
        P(("seq", "ctx"), None),
        P(("seq", "ctx"), None),
        P(("seq", "ctx"), None),
        P(("seq", "ctx"), None),
        P(),
    )
    return jax.shard_map(
        per_device,
        mesh=mesh,
        in_specs=placed,
        out_specs=(
            P(("seq", "ctx"), None),
            P(("seq", "ctx"), None),
            P(("seq", "ctx"), None),
            P("seq", None, None),
        ),
        check_vma=False,
    )
```

profile of v0, /device:TPU:448, one launch (start us, length us, event | category | flops | bytes accessed | tf_op | source)
XLA Modules:
  0.0 508.9 jit_solution(5333354857410361973)
XLA Ops:
  7.2 0.0 all-gather.5.cloned.1.call-start
  7.2 1.0 copy-done
  8.2 1.6 fusion.10
  9.8 2.1 convolution_convert_fusion.4
  11.9 0.0 all-gather.5.cloned.1.call-update
  11.9 0.0 all-gather.7.cloned.1.call-start
  12.0 1.3 copy.57
  13.3 1.6 fusion.11
  14.9 1.3 convolution_convert_fusion.2
  16.1 0.0 all-gather.7.cloned.1.call-update
  16.2 0.0 all-reduce.2.cloned.1.call-start
  16.2 1.6 fusion.1
  17.8 1.5 fusion.30
  19.3 1.3 fusion.31
  20.5 135.9 %all-gather.5.cloned.1.call-done = bf16[512,128,128]{2,1,0:T(8,128)(2,1)} async-done(((bf16[16,128,128]{2,1,0:T(8,128)(2,1)}), bf16[512,128,128]{2,1,0:T(8,128)(2,1)}) %all-gather.5.cloned.1.call-update) | async-done | bytes 16777232 | tf_op jit(solution)/shard_map/all_gather | solution.py:13
  156.4 0.1 broadcast_in_dim.17.clone
  156.6 1.5 fusion.9
  158.1 0.3 convolution_convert_fusion.1
  158.4 1.0 copy.47
  159.4 2.3 fusion.12
  161.7 140.8 %all-gather.7.cloned.1.call-done = bf16[512,128,128]{2,1,0:T(8,128)(2,1)} async-done(((bf16[16,128,128]{2,1,0:T(8,128)(2,1)}), bf16[512,128,128]{2,1,0:T(8,128)(2,1)}) %all-gather.7.cloned.1.call-update) | async-done | bytes 16777232 | tf_op jit(solution)/shard_map/all_gather | solution.py:13
  302.5 0.1 broadcast_in_dim.17.clone.1
  302.6 35.9 %while.23 = (s32[]{:T(128)}, bf16[16,128,128]{2,1,0:T(8,128)(2,1)S(1)}, s32[]{:T(128)}, bf16[32,16,128,128]{3,2,1,0:T(8,128)(2,1)}, s32[]{:T(128)}, /*index=5*/s32[]{:T(128)}, s32[]{:T(128)}, s32[]{:T(128)}) while((s32[]{:T(128)}, bf16[16,128,128]{2,1,0:T(8,128)(2,1)S(1)}, s32[]{:T(128)}, bf16[32,16,128,128]{3,2,1,0:T(8,128)(2,1)}, s32[]{:T(128)}, ...), condition=%wide.region_3.4_spmd, body=%wide.region_2.3_spmd.sunk | while | flops 262150 | bytes 1573007 | solution.py:20
  302.6 1.1 bitcast_add_fusion.5
  303.8 1.1 bitcast_add_fusion.5
  305.0 1.1 bitcast_add_fusion.5
  306.1 1.1 bitcast_add_fusion.5
  307.3 1.1 bitcast_add_fusion.5
  308.4 1.1 bitcast_add_fusion.5
  309.6 1.1 bitcast_add_fusion.5
  310.7 1.1 bitcast_add_fusion.5
  311.9 1.1 bitcast_add_fusion.5
  313.0 1.1 bitcast_add_fusion.5
  314.2 1.1 bitcast_add_fusion.5
  315.4 1.1 bitcast_add_fusion.5
  316.5 1.1 bitcast_add_fusion.5
  317.7 1.1 bitcast_add_fusion.5
  318.8 1.1 bitcast_add_fusion.5
  320.0 1.1 bitcast_add_fusion.5
  321.1 1.1 bitcast_add_fusion.5
  322.3 1.1 bitcast_add_fusion.5
  323.5 1.1 bitcast_add_fusion.5
  324.6 1.1 bitcast_add_fusion.5
  325.8 1.1 bitcast_add_fusion.5
  326.9 1.1 bitcast_add_fusion.5
  328.1 1.1 bitcast_add_fusion.5
  329.2 1.1 bitcast_add_fusion.5
  330.4 1.1 bitcast_add_fusion.5
  331.5 1.1 bitcast_add_fusion.5
  332.7 1.1 bitcast_add_fusion.5
  333.9 1.1 bitcast_add_fusion.5
  335.0 1.1 bitcast_add_fusion.5
  336.2 1.1 bitcast_add_fusion.5
  337.3 1.1 bitcast_add_fusion.5
  338.5 1.9 fusion.8
  340.4 1.1 convolution_convert_fusion
  341.4 2.0 copy.48
  343.5 2.5 fusion.7
  346.0 1.3 convolution_bitcast_fusion.1
  347.3 1.7 fusion.6
  349.0 1.0 copy.49
  350.0 149.8 %all-reduce.2.cloned.1.call-done = bf16[16,128,128]{1,2,0:T(8,128)(2,1)} async-done(((bf16[16,128,128]{1,2,0:T(8,128)(2,1)}), bf16[16,128,128]{1,2,0:T(8,128)(2,1)}) %all-reduce.2.cloned.1.call-update) | async-done | bytes 524304 | tf_op jit(solution)/shard_map/psum | solution.py:79
  499.9 1.1 convert_multiply_fusion
  501.0 1.3 copy.50
  (4 shorter events, 0.1 us)
Async XLA Ops:
  7.2 1.0 copy-start
  7.2 149.3 %all-gather.5.cloned.1.call-start = ((), (), s32[]{:S(2)}) async-start(), calls=%async_computation.1 | async-start | bytes 17301504 | tf_op jit(solution)/shard_map/all_gather | solution.py:13
  11.9 290.6 %all-gather.7.cloned.1.call-start = ((), (), s32[]{:S(2)}) async-start(), calls=%async_computation.2 | async-start | bytes 17301504 | tf_op jit(solution)/shard_map/all_gather | solution.py:13
  16.2 483.7 %all-reduce.2.cloned.1.call-start = ((), (), s32[]{:S(2)}) async-start(), calls=%async_computation | async-start | bytes 1048576 | tf_op jit(solution)/shard_map/psum | solution.py:79
Sparse Core Ops, SparseCore 0:
  12.1 144.3 all-gather.4
  160.2 142.2 all-gather.6
  346.1 153.7 all-reduce.1
where the time goes:
time: 515 us; the launch traced here: 509 us
  waiting for transfers between devices  427 us (83%)
  other arithmetic  36.3 us (7%)
  matrix products  23.4 us (5%)
  between operations  13.8 us (3%)
  local copies, waits for them, and re-layouts  7.86 us (2%)
    all_gather x2, waiting for transfers between devices, carried_in(): gathered = lax.all_gather(part, axis)  277 us
    psum x1, waiting for transfers between devices, per_device(): lax.psum(local_grad.astype(jnp.bfloat16), 'ctx').astype(jnp.float32)  150 us
    add x31, other arithmetic, add_states(): return earlier + later  35.1 us
  transfers between devices with their start and end apart: 3, of which 3 were waited for; matrix products, arithmetic and copies ran while one was open for 3% of the time, Pallas kernels for 0%

commit v1 on v0

v1 whole, which is shorter than its diff:
```python
import functools

import jax
import jax.numpy as jnp
from jax import lax
from jax.experimental import pallas as pl
from jax.experimental.pallas import tpu as pltpu
from jax.sharding import PartitionSpec as P

MESH = pl.DeviceIdType.MESH
F32 = jnp.float32
BF16 = jnp.bfloat16

NX = 4
NY = 8
HEADS = 16
QUARTER = HEADS // NX
CHUNKS = 2
PER = QUARTER // CHUNKS
HD = 128
OWNERS = (0, 4, 2, 6)


def mm(a, b, ca=1, cb=0):
    return lax.dot_general(a, b, (((ca,), (cb,)), ((), ())), preferred_element_type=F32)


def kernel(
    q_in, k_in, v_in, g_in, f_in,
    q_out, k_out, v_out, z_out,
    q, k, v, g, f, dq, dk, dv,
    sent, got, y_sent, y_got, total, z_row, w_row,
    col, col_z, carry, carried, w_col, z_all,
    out_send, fin, h_mat, kh, aq, ak, av,
    in_sem, out_sem, z_sem,
    p1s, p1r, ys, yr, p2s, p2r, z2s, z2r, p3s, p3r, z3s, z3r, p4s, p4r, z4s, z4r,
):
    me = lax.axis_index("ctx")
    y = me // NX
    x = lax.rem(me, NX)
    mine_j = lax.rem(y // 2, 2) * 2 + y // 4
    is_owner = lax.rem(y, 2) == 0

    def at_x(d):
        return lax.rem(x + d + NX, NX)

    def at_y(d):
        return lax.rem(y + d + NY, NY)

    def place(py, px):
        return {"ctx": py * NX + px}

    def remote(src, dst, ssem, rsem, py, px):
        return pltpu.make_async_remote_copy(
            src_ref=src, dst_ref=dst, send_sem=ssem, recv_sem=rsem,
            device_id=place(py, px), device_id_type=MESH,
        )

    loads = [
        pltpu.make_async_copy(a, b, in_sem.at[i])
        for i, (a, b) in enumerate(((k_in, k), (v_in, v), (q_in, q), (g_in, g), (f_in, f)))
    ]
    for load in loads:
        load.start()

    barrier = pltpu.get_barrier_semaphore()
    for d in range(1, NX):
        pl.semaphore_signal(barrier, inc=1, device_id=place(y, at_x(d)), device_id_type=MESH)
    for d in range(1, NY):
        pl.semaphore_signal(barrier, inc=1, device_id=place(at_y(d), x), device_id_type=MESH)
    for load in loads[:4]:
        load.wait()
    pl.semaphore_wait(barrier, NX + NY - 2)

    def cols(h):
        return pl.ds(pl.multiple_of(h * HD, HD), HD)

    def p1(c, d):
        js = pl.ds(c * PER, PER)
        return remote(sent.at[at_x(d), js], got.at[x, js], p1s.at[c, d - 1], p1r.at[c, d - 1], y, at_x(d))

    def p1_in(c, d):
        js = pl.ds(c * PER, PER)
        return remote(sent.at[at_x(d), js], got.at[at_x(-d), js], p1s.at[c, d - 1], p1r.at[c, d - 1], y, at_x(d))

    def py_(c, d):
        js = pl.ds(c * PER, PER)
        return remote(y_sent.at[at_x(d), js], y_got.at[x, js], ys.at[c, d - 1], yr.at[c, d - 1], y, at_x(d))

    def py_in(c, d):
        js = pl.ds(c * PER, PER)
        return remote(y_sent.at[at_x(d), js], y_got.at[at_x(-d), js], ys.at[c, d - 1], yr.at[c, d - 1], y, at_x(d))

    def p2(j):
        return remote(total.at[j], col.at[y], p2s.at[j], p2r.at[y], OWNERS[j], x)

    def p2_in(d):
        return remote(total.at[0], col.at[at_y(d)], p2s.at[0], p2r.at[at_y(d)], at_y(d), x)

    def z2(j):
        return remote(z_row.at[j], col_z.at[y], z2s.at[j], z2r.at[y], OWNERS[j], x)

    def z2_in(d):
        return remote(z_row.at[0], col_z.at[at_y(d)], z2s.at[0], z2r.at[at_y(d)], at_y(d), x)

    def p3(d):
        return remote(carry.at[at_y(d)], carried.at[mine_j], p3s.at[d - 1], p3r.at[mine_j], at_y(d), x)

    def p3_in(j):
        return remote(carry.at[0], carried.at[j], p3s.at[0], p3r.at[j], OWNERS[j], x)

    def z3(d):
        head = x * QUARTER + mine_j
        return remote(z_all.at[head], z_all.at[head], z3s.at[d - 1], z3r.at[mine_j], at_y(d), x)

    def z3_in(j):
        head = x * QUARTER + j
        return remote(z_all.at[head], z_all.at[head], z3s.at[0], z3r.at[j], OWNERS[j], x)

    def p4(c, d):
        return remote(
            out_send.at[at_x(d), pl.ds(c * PER, PER)], fin.at[pl.ds(x * QUARTER + c * PER, PER)],
            p4s.at[c, d - 1], p4r.at[c, d - 1], y, at_x(d),
        )

    def p4_in(c, d):
        return remote(
            out_send.at[at_x(d), pl.ds(c * PER, PER)], fin.at[pl.ds(at_x(-d) * QUARTER + c * PER, PER)],
            p4s.at[c, d - 1], p4r.at[c, d - 1], y, at_x(d),
        )

    def z4(c, d):
        hs = pl.ds(x * QUARTER + c * PER, PER)
        return remote(z_all.at[hs], z_all.at[hs], z4s.at[c, d - 1], z4r.at[c, d - 1], y, at_x(d))

    def z4_in(c, d):
        hs = pl.ds(at_x(-d) * QUARTER + c * PER, PER)
        return remote(z_all.at[hs], z_all.at[hs], z4s.at[c, d - 1], z4r.at[c, d - 1], y, at_x(d))

    order = (2, 1, 3)
    for c in range(CHUNKS):
        for d in order + (0,):
            xo = at_x(d)
            for j in range(c * PER, c * PER + PER):
                hc = cols(xo * QUARTER + j)
                ks = mm(v[:, hc], k[:, hc], 0, 0).astype(BF16)
                gs = mm(q[:, hc], g[:, hc], 0, 0).astype(BF16)
                if d:
                    sent[xo, j, 0] = ks
                    sent[xo, j, 1] = gs
                else:
                    got[x, j, 0] = ks
                    got[x, j, 1] = gs
            if d:
                p1(c, d).start()

    loads[4].wait()
    rows = lax.broadcasted_iota(jnp.int32, (HD, HD), 0)
    columns = lax.broadcasted_iota(jnp.int32, (HD, HD), 1)
    lower = rows >= columns
    upper = rows <= columns

    def local(h):
        hc = cols(h)
        qh, kh_in, vh, gh = q[:, hc], k[:, hc], v[:, hc], g[:, hc]
        fh = f[h]
        hm = mm(fh, fh, 1, 1).astype(BF16)
        h_mat[h] = hm
        khm = mm(kh_in, hm).astype(BF16)
        kh[h] = khm
        scores_t = jnp.where(upper, mm(khm, qh, 1, 1), 0.0).astype(BF16)
        mixing = jnp.where(lower, mm(gh, vh, 1, 1), 0.0).astype(BF16)
        mixing_t = jnp.where(upper, mm(vh, gh, 1, 1), 0.0).astype(BF16)
        a = mm(mixing, kh_in)
        aq[h] = a
        ak[h] = mm(mixing_t, qh)
        av[h] = mm(scores_t, gh)
        return mm(qh, a.astype(BF16), 0, 0).astype(BF16)

    for c in range(CHUNKS):
        for d in order + (0,):
            xo = at_x(d)
            for j in range(c * PER, c * PER + PER):
                part = local(xo * QUARTER + j)
                if d:
                    y_sent[xo, j] = part
                else:
                    y_got[x, j] = part
            if d:
                py_(c, d).start()

    def sums(j):
        ks = [got[i, j, 0].astype(F32) for i in range(NX)]
        gs = [got[i, j, 1].astype(F32) for i in range(NX)]
        before = [None, ks[0]]
        for i in range(1, NX):
            before.append(before[-1] + ks[i])
        after = [None, gs[NX - 1]]
        for i in range(NX - 2, -1, -1):
            after.append(after[-1] + gs[i])
        return before, after

    for c in range(CHUNKS):
        for d in order:
            p1_in(c, d).wait_recv()
        for j in range(c * PER, c * PER + PER):
            before, after = sums(j)
            total[j, 0] = before[NX].astype(BF16)
            total[j, 1] = after[NX].astype(BF16)

            @pl.when(y != OWNERS[j])
            def _():
                p2(j).start()

            @pl.when(y == OWNERS[j])
            def _():
                col[y] = total[j]

            w = mm(got[1, j, 1], before[1].astype(BF16))
            for i in range(2, NX):
                w += mm(got[i, j, 1], before[i].astype(BF16))
            w_row[j] = w
    for c in range(CHUNKS):
        for d in order:
            py_in(c, d).wait_recv()
        for j in range(c * PER, c * PER + PER):
            w = w_row[j]
            for i in range(NX):
                w += y_got[i, j].astype(F32)
            z_row[j] = w.astype(BF16)

            @pl.when(y != OWNERS[j])
            def _():
                z2(j).start()

            @pl.when(y == OWNERS[j])
            def _():
                col_z[y] = z_row[j]

    for c in range(CHUNKS):

        @pl.when(is_owner & (mine_j // PER == c))
        def _():
            for d in range(1, NY):
                p2_in(d).wait_recv()
            acc = jnp.zeros((HD, HD), F32)
            w = jnp.zeros((HD, HD), F32)
            for i in range(NY):
                low = acc.astype(BF16)
                carry[i, 0] = low
                if i:
                    w += mm(col[i, 1], low)
                acc = acc + col[i, 0].astype(F32)
            acc = jnp.zeros((HD, HD), F32)
            for i in range(NY - 1, -1, -1):
                carry[i, 1] = acc.astype(BF16)
                acc = acc + col[i, 1].astype(F32)
            for d in (4, 3, 5, 2, 6, 1, 7):
                p3(d).start()
            carried[mine_j] = carry[y]
            for d in range(1, NY):
                z2_in(d).wait_recv()
            for i in range(NY):
                w += col_z[i].astype(F32)
            w = w + w.T
            z_all[x * QUARTER + mine_j] = w.astype(BF16)
            for d in (4, 3, 5, 2, 6, 1, 7):
                z3(d).start()

        for j in range(c * PER, c * PER + PER):

            @pl.when(y != OWNERS[j])
            def _():
                p3_in(j).wait_recv()

            before, after = sums(j)
            pre = carried[j, 0].astype(F32)
            suf = carried[j, 1].astype(F32)
            for i in range(NX):
                out_send[i, j, 0] = (pre if i == 0 else pre + before[i]).astype(BF16)
                back = NX - 1 - i
                out_send[i, j, 1] = (suf if back == 0 else suf + after[back]).astype(BF16)
        for d in order:
            p4(c, d).start()
        fin[pl.ds(x * QUARTER + c * PER, PER)] = out_send[x, pl.ds(c * PER, PER)]
        for j in range(c * PER, c * PER + PER):

            @pl.when(y != OWNERS[j])
            def _():
                z3_in(j).wait_recv()

        for d in order:
            z4(c, d).start()

    def finish(h):
        hc = cols(h)
        pre_t = fin[h, 0]
        suf = fin[h, 1]
        hm = h_mat[h]
        a = (aq[h] + mm(g[:, hc], pre_t)).astype(BF16)
        dq[:, hc] = mm(a, hm).astype(BF16)
        b = (ak[h] + mm(v[:, hc], suf, 1, 1)).astype(BF16)
        dk[:, hc] = mm(b, hm).astype(BF16)
        dv[:, hc] = (av[h] + mm(kh[h], suf)).astype(BF16)

    outs = []
    for c in range(CHUNKS):
        for n, d in enumerate((0, 1, 3, 2)):
            if d:
                p4_in(c, d).wait_recv()
            xo = at_x(-d)
            for j in range(c * PER, c * PER + PER):
                finish(xo * QUARTER + j)
            part = pl.ds(pl.multiple_of((xo * QUARTER + c * PER) * HD, PER * HD), PER * HD)
            for i, (a, b) in enumerate(((dq, q_out), (dk, k_out), (dv, v_out))):
                copy = pltpu.make_async_copy(a.at[:, part], b.at[:, part], out_sem.at[c, n, i])
                copy.start()
                outs.append(copy)
    for c in range(CHUNKS):
        for d in order:
            z4_in(c, d).wait_recv()
    z_copy = pltpu.make_async_copy(z_all, z_out, z_sem)
    z_copy.start()

    for c in range(CHUNKS):
        for d in order:
            p1(c, d).wait_send()
            py_(c, d).wait_send()
            p4(c, d).wait_send()
            z4(c, d).wait_send()
    for j in range(QUARTER):

        @pl.when(y != OWNERS[j])
        def _():
            p2(j).wait_send()
            z2(j).wait_send()

    @pl.when(is_owner)
    def _():
        for d in range(1, NY):
            p3(d).wait_send()
            z3(d).wait_send()

    for copy in outs:
        copy.wait()
    z_copy.wait()


def per_device(queries, key_rows, values, out_grad, feature_map):
    tokens, width = queries.shape
    dma = pltpu.SemaphoreType.DMA
    state = (HD, HD)
    flat = jax.ShapeDtypeStruct((tokens, width), BF16)
    rows = (tokens, width)
    query_grad, key_grad, value_grad, z = pl.pallas_call(
        kernel,
        out_shape=(flat, flat, flat, jax.ShapeDtypeStruct((HEADS,) + state, BF16)),
        in_specs=[pl.BlockSpec(memory_space=pl.ANY)] * 5,
        out_specs=[pl.BlockSpec(memory_space=pl.ANY)] * 4,
        scratch_shapes=[
            pltpu.VMEM(rows, BF16), pltpu.VMEM(rows, BF16), pltpu.VMEM(rows, BF16), pltpu.VMEM(rows, BF16),
            pltpu.VMEM((HEADS,) + state, BF16),
            pltpu.VMEM(rows, BF16), pltpu.VMEM(rows, BF16), pltpu.VMEM(rows, BF16),
            pltpu.VMEM((NX, QUARTER, 2) + state, BF16),
            pltpu.VMEM((NX, QUARTER, 2) + state, BF16),
            pltpu.VMEM((NX, QUARTER) + state, BF16),
            pltpu.VMEM((NX, QUARTER) + state, BF16),
            pltpu.VMEM((QUARTER, 2) + state, BF16),
            pltpu.VMEM((QUARTER,) + state, BF16),
            pltpu.VMEM((QUARTER,) + state, F32),
            pltpu.VMEM((NY, 2) + state, BF16),
            pltpu.VMEM((NY,) + state, BF16),
            pltpu.VMEM((NY, 2) + state, BF16),
            pltpu.VMEM((QUARTER, 2) + state, BF16),
            pltpu.VMEM(state, F32),
            pltpu.VMEM((HEADS,) + state, BF16),
            pltpu.VMEM((NX, QUARTER, 2) + state, BF16),
            pltpu.VMEM((HEADS, 2) + state, BF16),
            pltpu.VMEM((HEADS,) + state, BF16),
            pltpu.VMEM((HEADS,) + state, BF16),
            pltpu.VMEM((HEADS,) + state, F32), pltpu.VMEM((HEADS,) + state, F32), pltpu.VMEM((HEADS,) + state, F32),
            dma((5,)), dma((CHUNKS, NX, 3)), dma,
            dma((CHUNKS, 3)), dma((CHUNKS, 3)), dma((CHUNKS, 3)), dma((CHUNKS, 3)),
            dma((QUARTER,)), dma((NY,)), dma((QUARTER,)), dma((NY,)),
            dma((NY - 1,)), dma((QUARTER,)), dma((NY - 1,)), dma((QUARTER,)),
            dma((CHUNKS, 3)), dma((CHUNKS, 3)), dma((CHUNKS, 3)), dma((CHUNKS, 3)),
        ],
        compiler_params=pltpu.CompilerParams(
            collective_id=0, has_side_effects=True, vmem_limit_bytes=48 * 1024 * 1024
        ),
    )(queries, key_rows, values, out_grad, feature_map)
    map_grad = jnp.einsum("hcd,hde->hce", z, feature_map, preferred_element_type=F32) * (
        1.0 / (tokens * lax.axis_size("ctx")) ** 0.5
    )
    return query_grad, key_grad, value_grad, map_grad


def solution(mesh):
    placed = P(("seq", "ctx"), None)
    return jax.shard_map(
        per_device,
        mesh=mesh,
        in_specs=(placed, placed, placed, placed, P()),
        out_specs=(placed, placed, placed, P("seq", None, None)),
        check_vma=False,
    )
```

time: 515 us -> 68.6 us (0.13); the launches traced: 509 us -> 68.3 us
  waiting for transfers between devices: 427 us -> 0 us
  Pallas kernels: 0 us -> 58.8 us
  other arithmetic: 36.3 us -> 0 us
  matrix products: 23.4 us -> 1.26 us
  between operations: 13.8 us -> 0.65 us
    all_gather x2 -> x0, waiting for transfers between devices: 277 us -> none  [carried_in(): gathered = lax.all_gather(part, axis)]
    psum x1 -> x0, waiting for transfers between devices: 150 us -> none  [per_device(): lax.psum(local_grad.astype(jnp.bfloat16), 'ctx').astype(jnp.float32)]
    pallas_call x0 -> x1, Pallas kernels: none -> 58.8 us  [per_device(): pl.pallas_call(kernel, out_shape=(flat, flat, flat, jax.ShapeDtypeStruct(...]
    add x31 -> x0, other arithmetic: 35.1 us -> none  [add_states(): return earlier + later]
    dot_general x15 -> x1, matrix products: 23.4 us -> 1.26 us  [per_device(): jnp.einsum('hcd,hde->hce', z, feature_map, preferred_element_type=F32)]
  transfers between devices with their start and end apart: 3 -> 0, of which waited for: 3 -> 0; matrix products, arithmetic and copies ran while one was open for 3% -> 0% of each run, Pallas kernels for 0% -> 0%
where the time goes in v1:
time: 68.6 us; the launch traced here: 68.3 us
  Pallas kernels  58.8 us (86%)
  local copies, waits for them, and re-layouts  7.58 us (11%)
  matrix products  1.26 us (2%)
    pallas_call x1, Pallas kernels, per_device(): pl.pallas_call(kernel, out_shape=(flat, flat, flat, jax.ShapeDtypeStruct(...  58.8 us
    unnamed x13, local copies, waits for them, and re-layouts  7.58 us

profile of v1, /device:TPU:448, one launch (start us, length us, event | category | flops | bytes accessed | tf_op | source)
XLA Modules:
  0.0 68.3 jit_solution(6574416369783810625)
XLA Ops:
  0.6 0.0 copy-start
  0.6 1.0 %copy-done = bf16[16,128,128]{2,1,0:T(8,128)(2,1)S(1)} copy-done((bf16[16,128,128]{2,1,0:T(8,128)(2,1)S(1)}, bf16[16,128,128]{2,1,0:T(8,128)(2,1)}, u32[]{:S(2)}) %copy-start) | copy-done | bytes 524312
  1.7 0.0 copy-start.1
  1.7 1.0 %copy-done.1 = bf16[128,2048]{1,0:T(8,128)(2,1)S(1)} copy-done((bf16[128,2048]{1,0:T(8,128)(2,1)S(1)}, bf16[128,2048]{1,0:T(8,128)(2,1)}, u32[]{:S(2)}) %copy-start.1) | copy-done | bytes 524312
  2.7 0.0 copy-start.2
  2.7 1.0 %copy-done.2 = bf16[128,2048]{1,0:T(8,128)(2,1)S(1)} copy-done((bf16[128,2048]{1,0:T(8,128)(2,1)S(1)}, bf16[128,2048]{1,0:T(8,128)(2,1)}, u32[]{:S(2)}) %copy-start.2) | copy-done | bytes 524312
  3.8 0.0 copy-start.3
  3.8 1.0 %copy-done.3 = bf16[128,2048]{1,0:T(8,128)(2,1)S(1)} copy-done((bf16[128,2048]{1,0:T(8,128)(2,1)S(1)}, bf16[128,2048]{1,0:T(8,128)(2,1)}, u32[]{:S(2)}) %copy-start.3) | copy-done | bytes 524312
  4.8 0.0 copy-start.4
  4.8 1.0 %copy-done.4 = bf16[128,2048]{1,0:T(8,128)(2,1)S(1)} copy-done((bf16[128,2048]{1,0:T(8,128)(2,1)S(1)}, bf16[128,2048]{1,0:T(8,128)(2,1)}, u32[]{:S(2)}) %copy-start.4) | copy-done | bytes 524312
  5.8 58.8 %shard_map.84 = (bf16[128,2048]{1,0:T(8,128)(2,1)S(1)}, bf16[128,2048]{1,0:T(8,128)(2,1)S(1)}, bf16[128,2048]{1,0:T(8,128)(2,1)S(1)}, bf16[16,128,128]{2,1,0:T(8,128)(2,1)S(1)}) custom-call(bf16[128,2048]{1,0:T(8,128)(2,1)S(1)} %copy-done.1, bf16[128,2048]{1,0:T(8,128)(2,1)S(1)} %copy-done.2, bf16[128,2048]{1,0:T(8,128)(2,1)S(1)} %copy-done.3, ...), custom_call_target="tpu_custom_call" | custom-call | tf_op jit(solution)/shard_map/pallas_call | solution.py:355
  64.6 1.3 %convolution_multiply_fusion = f32[16,128,128]{2,1,0:T(8,128)} fusion(bf16[16,128,128]{2,1,0:T(8,128)(2,1)S(1)} %get-tuple-element.11, bf16[16,128,128]{2,1,0:T(8,128)(2,1)S(1)} %copy-done), kind=kOutput, calls=%fused_computation | convolution fusion | flops 67371008 | bytes 2097152 | tf_op jit(solution)/shard_map/hcd,hde->hce/dot_general | solution.py:392
  65.9 0.8 %copy.12 = bf16[128,2048]{1,0:T(8,128)(2,1)} copy(bf16[128,2048]{1,0:T(8,128)(2,1)S(1)} %get-tuple-element.16) | data formatting | bytes 1048576
  66.7 0.8 %copy.13 = bf16[128,2048]{1,0:T(8,128)(2,1)} copy(bf16[128,2048]{1,0:T(8,128)(2,1)S(1)} %get-tuple-element.17) | data formatting | bytes 1048576
  67.5 0.8 %copy.14 = bf16[128,2048]{1,0:T(8,128)(2,1)} copy(bf16[128,2048]{1,0:T(8,128)(2,1)S(1)} %get-tuple-element.18) | data formatting | bytes 1048576
Async XLA Ops:
  0.6 1.0 %copy-start = (bf16[16,128,128]{2,1,0:T(8,128)(2,1)S(1)}, bf16[16,128,128]{2,1,0:T(8,128)(2,1)}, u32[]{:S(2)}) copy-start(bf16[16,128,128]{2,1,0:T(8,128)(2,1)} %f_in.1) | copy-start | bytes 1572868
  1.7 1.0 %copy-start.1 = (bf16[128,2048]{1,0:T(8,128)(2,1)S(1)}, bf16[128,2048]{1,0:T(8,128)(2,1)}, u32[]{:S(2)}) copy-start(bf16[128,2048]{1,0:T(8,128)(2,1)} %q_in.1) | copy-start | bytes 1572868
  2.7 1.0 %copy-start.2 = (bf16[128,2048]{1,0:T(8,128)(2,1)S(1)}, bf16[128,2048]{1,0:T(8,128)(2,1)}, u32[]{:S(2)}) copy-start(bf16[128,2048]{1,0:T(8,128)(2,1)} %k_in.1) | copy-start | bytes 1572868
  3.8 1.0 %copy-start.3 = (bf16[128,2048]{1,0:T(8,128)(2,1)S(1)}, bf16[128,2048]{1,0:T(8,128)(2,1)}, u32[]{:S(2)}) copy-start(bf16[128,2048]{1,0:T(8,128)(2,1)} %v_in.1) | copy-start | bytes 1572868
  4.8 1.0 %copy-start.4 = (bf16[128,2048]{1,0:T(8,128)(2,1)S(1)}, bf16[128,2048]{1,0:T(8,128)(2,1)}, u32[]{:S(2)}) copy-start(bf16[128,2048]{1,0:T(8,128)(2,1)} %g_in.1) | copy-start | bytes 1572868

commit v2 on v1

v2 whole, which is shorter than its diff:
```python
import functools
import math

import jax
import jax.numpy as jnp
from jax import lax
from jax.experimental import pallas as pl
from jax.experimental.pallas import tpu as pltpu
from jax.sharding import PartitionSpec as P

MESH = pl.DeviceIdType.MESH
F32 = jnp.float32
BF16 = jnp.bfloat16

NX = 4
NY = 8
HEADS = 16
QUARTER = HEADS // NX
CHUNKS = 4
PER = QUARTER // CHUNKS
HD = 128
SLICE = HD // NY


def mm(a, b, ca=1, cb=0):
    return lax.dot_general(a, b, (((ca,), (cb,)), ((), ())), preferred_element_type=F32)


def kernel(
    q_in, k_in, v_in, g_in, f_in,
    q_out, k_out, v_out, z_out,
    q, k, v, g, f, dq, dk, dv,
    sent, got, y_sent, y_got, total, col, carry, carried,
    w_row, z_row, col_z, z_part, z_full, z_all,
    out_send, fin, h_mat, kh, aq, ak, av,
    in_sem, out_sem, z_sem,
    p1s, p1r, ys, yr, p2s, p2r, p3s, p3r, p4s, p4r, z2s, z2r, z3s, z3r, z4s, z4r,
):
    me = lax.axis_index("ctx")
    y = me // NX
    x = lax.rem(me, NX)

    def at_x(d):
        return lax.rem(x + d + NX, NX)

    def at_y(d):
        return lax.rem(y + d + NY, NY)

    def place(py, px):
        return {"ctx": py * NX + px}

    loads = [
        pltpu.make_async_copy(a, b, in_sem.at[i])
        for i, (a, b) in enumerate(((k_in, k), (v_in, v), (q_in, q), (g_in, g), (f_in, f)))
    ]
    for load in loads:
        load.start()

    barrier = pltpu.get_barrier_semaphore()
    for d in range(1, NX):
        pl.semaphore_signal(barrier, inc=1, device_id=place(y, at_x(d)), device_id_type=MESH)
    for d in range(1, NY):
        pl.semaphore_signal(barrier, inc=1, device_id=place(at_y(d), x), device_id_type=MESH)
    for load in loads[:4]:
        load.wait()
    pl.semaphore_wait(barrier, NX + NY - 2)

    def cols(h, n=1):
        return pl.ds(pl.multiple_of(h * HD, HD), n * HD)

    def rows_of(i):
        return pl.ds(pl.multiple_of(i * SLICE, SLICE), SLICE)

    def heads_of(c):
        return range(c * PER, c * PER + PER)

    def along_x(src, dst, ssem, rsem, c, d, into):
        return pltpu.make_async_remote_copy(
            src_ref=src(at_x(d)), dst_ref=dst(at_x(-d) if into else x),
            send_sem=ssem.at[c, d - 1], recv_sem=rsem.at[c, d - 1],
            device_id=place(y, at_x(d)), device_id_type=MESH,
        )

    def along_y(src, dst, ssem, rsem, c, d, into):
        return pltpu.make_async_remote_copy(
            src_ref=src(at_y(d)), dst_ref=dst(at_y(-d) if into else y),
            send_sem=ssem.at[c, d - 1], recv_sem=rsem.at[c, d - 1],
            device_id=place(at_y(d), x), device_id_type=MESH,
        )

    def p1(c, d, into=False):
        js = pl.ds(c * PER, PER)
        return along_x(lambda i: sent.at[i, js], lambda i: got.at[i, js], p1s, p1r, c, d, into)

    def p_y(c, d, into=False):
        js = pl.ds(c * PER, PER)
        return along_x(lambda i: y_sent.at[i, js], lambda i: y_got.at[i, js], ys, yr, c, d, into)

    def p2(c, d, into=False):
        js = pl.ds(c * PER, PER)
        return along_y(lambda i: total.at[js, :, rows_of(i)], lambda i: col.at[i, js], p2s, p2r, c, d, into)

    def p3(c, d, into=False):
        js = pl.ds(c * PER, PER)
        return along_y(lambda i: carry.at[i, js], lambda i: carried.at[js, :, rows_of(i)], p3s, p3r, c, d, into)

    def p4(c, d, into=False):
        js = pl.ds(c * PER, PER)
        return along_x(
            lambda i: out_send.at[i, js], lambda i: fin.at[pl.ds(i * QUARTER + c * PER, PER)], p4s, p4r, c, d, into
        )

    def z2(c, d, into=False):
        js = pl.ds(c * PER, PER)
        return along_y(lambda i: z_row.at[js, rows_of(i)], lambda i: col_z.at[i, js], z2s, z2r, c, d, into)

    def z3(c, d, into=False):
        js = pl.ds(c * PER, PER)
        return along_y(lambda i: z_part.at[js], lambda i: z_full.at[js, rows_of(i)], z3s, z3r, c, d, into)

    def z4(c, d, into=False):
        def hs(i):
            return z_all.at[pl.ds(i * QUARTER + c * PER, PER)]

        return along_x(lambda i: hs(x), hs, z4s, z4r, c, d, into)

    x_order = (2, 1, 3)
    y_order = (4, 3, 5, 2, 6, 1, 7)

    def states(c, send=True):
        for d in x_order + (0,):
            xo = at_x(d)
            for j in heads_of(c):
                hc = cols(xo * QUARTER + j)
                ks = mm(v[:, hc], k[:, hc], 0, 0).astype(BF16)
                gs = mm(g[:, hc], q[:, hc], 0, 0).astype(BF16)
                if d:
                    sent[xo, j, 0] = ks
                    sent[xo, j, 1] = gs
                else:
                    got[x, j, 0] = ks
                    got[x, j, 1] = gs
            if d and send:
                p1(c, d).start()

    def send_states(c):
        for d in x_order:
            p1(c, d).start()

    rows = lax.broadcasted_iota(jnp.int32, (HD, HD), 0)
    columns = lax.broadcasted_iota(jnp.int32, (HD, HD), 1)
    lower = rows >= columns
    upper = rows <= columns

    def local(h):
        hc = cols(h)
        qh, kh_in, vh, gh = q[:, hc], k[:, hc], v[:, hc], g[:, hc]
        fh = f[h]
        hm = mm(fh, fh, 1, 1).astype(BF16)
        h_mat[h] = hm
        khm = mm(kh_in, hm).astype(BF16)
        kh[h] = khm
        scores_t = jnp.where(upper, mm(khm, qh, 1, 1), 0.0).astype(BF16)
        mixing = jnp.where(lower, mm(gh, vh, 1, 1), 0.0).astype(BF16)
        mixing_t = jnp.where(upper, mm(vh, gh, 1, 1), 0.0).astype(BF16)
        a = mm(mixing, kh_in)
        aq[h] = a
        ak[h] = mm(mixing_t, qh)
        av[h] = mm(scores_t, gh)
        return mm(qh, a.astype(BF16), 0, 0).astype(BF16)

    def block_work(c, d):
        xo = at_x(d)
        for j in heads_of(c):
            part = local(xo * QUARTER + j)
            if d:
                y_sent[xo, j] = part
            else:
                y_got[x, j] = part

    def send_y(c):
        for d in x_order:
            p_y(c, d).start()

    def sums(j):
        ks = [got[i, j, 0].astype(F32) for i in range(NX)]
        gs = [got[i, j, 1].astype(F32) for i in range(NX)]
        before = [None, ks[0]]
        for i in range(1, NX):
            before.append(before[-1] + ks[i])
        after = [None, gs[NX - 1]]
        for i in range(NX - 2, -1, -1):
            after.append(after[-1] + gs[i])
        return before, after

    def row_sums(c):
        for d in x_order:
            p1(c, d, True).wait_recv()
        for j in heads_of(c):
            before, after = sums(j)
            total[j, 0] = before[NX].astype(BF16)
            total[j, 1] = after[NX].astype(BF16)
            col[y, j] = total[j, :, rows_of(y)]
        for d in y_order:
            p2(c, d).start()

    def scan(c):
        for d in y_order:
            p2(c, d, True).wait_recv()
        for j in heads_of(c):
            acc = jnp.zeros((SLICE, HD), F32)
            for i in range(NY):
                carry[i, j, 0] = acc.astype(BF16)
                acc = acc + col[i, j, 0].astype(F32)
            acc = jnp.zeros((SLICE, HD), F32)
            for i in range(NY - 1, -1, -1):
                carry[i, j, 1] = acc.astype(BF16)
                acc = acc + col[i, j, 1].astype(F32)
            carried[j, :, rows_of(y)] = carry[y, j]
        for d in y_order:
            p3(c, d).start()

    def row_back(c):
        for d in y_order:
            p3(c, d, True).wait_recv()
        for j in heads_of(c):
            before, after = sums(j)
            pre = carried[j, 0].astype(F32)
            suf = carried[j, 1].astype(F32)
            for i in range(NX):
                out_send[i, j, 0] = (pre if i == 0 else pre + before[i]).astype(BF16)
                back = NX - 1 - i
                out_send[i, j, 1] = (suf if back == 0 else suf + after[back]).astype(BF16)
        for d in x_order:
            p4(c, d).start()
        fin[pl.ds(x * QUARTER + c * PER, PER)] = out_send[x, pl.ds(c * PER, PER)]

    def row_w(c):
        for j in heads_of(c):
            before, _ = sums(j)
            w = mm(got[1, j, 1], before[1].astype(BF16), 0, 0)
            for i in range(2, NX):
                w += mm(got[i, j, 1], before[i].astype(BF16), 0, 0)
            w_row[j] = w

    def row_z(c):
        for d in x_order:
            p_y(c, d, True).wait_recv()
        for j in heads_of(c):
            later = col[:, j, 1].reshape(HD, HD)
            w = w_row[j] + mm(later, carry[:, j, 0].reshape(HD, HD), 0, 0)
            for i in range(NX):
                w += y_got[i, j].astype(F32)
            z_row[j] = w.astype(BF16)
            col_z[y, j] = z_row[j, rows_of(y)]
        for d in y_order:
            z2(c, d).start()

    def col_z_sum(c):
        for d in y_order:
            z2(c, d, True).wait_recv()
        for j in heads_of(c):
            w = col_z[0, j].astype(F32)
            for i in range(1, NY):
                w += col_z[i, j].astype(F32)
            z_part[j] = w.astype(BF16)
            z_full[j, rows_of(y)] = z_part[j]
        for d in y_order:
            z3(c, d).start()

    def row_z_back(c):
        for d in y_order:
            z3(c, d, True).wait_recv()
        for j in heads_of(c):
            w = z_full[j].astype(F32)
            z_all[x * QUARTER + j] = (w + w.T).astype(BF16)
        for d in x_order:
            z4(c, d).start()

    def finish_head(h):
        hc = cols(h)
        pre_t = fin[h, 0]
        suf = fin[h, 1]
        hm = h_mat[h]
        a = (aq[h] + mm(g[:, hc], pre_t)).astype(BF16)
        dq[:, hc] = mm(a, hm).astype(BF16)
        b = (ak[h] + mm(v[:, hc], suf)).astype(BF16)
        dk[:, hc] = mm(b, hm).astype(BF16)
        dv[:, hc] = (av[h] + mm(kh[h], suf, 1, 1)).astype(BF16)

    outs = []

    def finish(c):
        for n, d in enumerate((0, 1, 3, 2)):
            if d:
                p4(c, d, True).wait_recv()
            xo = at_x(-d)
            for j in heads_of(c):
                finish_head(xo * QUARTER + j)
            part = cols(xo * QUARTER + c * PER, PER)
            for i, (a, b) in enumerate(((dq, q_out), (dk, k_out), (dv, v_out))):
                copy = pltpu.make_async_copy(a.at[:, part], b.at[:, part], out_sem.at[c, n, i])
                copy.start()
                outs.append(copy)

    blocks = [(c, d) for c in range(CHUNKS) for d in x_order + (0,)]

    def block_span(lo, hi):
        for c, d in blocks[lo:hi]:
            block_work(c, d)

    states(0)
    states(1, False)
    states(2, False)
    states(3, False)
    loads[4].wait()
    block_span(0, 1)
    send_states(1)
    block_span(1, 5)
    send_states(2)
    row_sums(0)
    block_span(5, 8)
    send_states(3)
    row_sums(1)
    block_span(8, 12)
    scan(0)
    row_sums(2)
    send_y(0)
    block_span(12, 14)
    send_y(1)
    scan(1)
    row_sums(3)
    send_y(2)
    block_span(14, 16)
    send_y(3)
    row_back(0)
    scan(2)
    row_w(0)
    row_z(0)
    row_back(1)
    scan(3)
    row_w(1)
    row_z(1)
    row_w(2)
    row_z(2)
    row_w(3)
    row_z(3)
    row_back(2)
    col_z_sum(0)
    row_back(3)
    col_z_sum(1)
    finish(0)
    col_z_sum(2)
    col_z_sum(3)
    row_z_back(0)
    finish(1)
    row_z_back(1)
    finish(2)
    row_z_back(2)
    row_z_back(3)
    finish(3)
    for c in range(CHUNKS):
        for d in x_order:
            z4(c, d, True).wait_recv()
    z_copy = pltpu.make_async_copy(z_all, z_out, z_sem)
    z_copy.start()

    for c in range(CHUNKS):
        for d in x_order:
            for p in (p1, p_y, p4, z4):
                p(c, d).wait_send()
        for d in y_order:
            for p in (p2, p3, z2, z3):
                p(c, d).wait_send()
    for copy in outs:
        copy.wait()
    z_copy.wait()


def emit(q_in, k_in, v_in, z, f, q_out, k_out, v_out, m_out, m, sem, m_sem, scale):
    copies = [
        pltpu.make_async_copy(a, b, sem.at[i])
        for i, (a, b) in enumerate(((q_in, q_out), (k_in, k_out), (v_in, v_out)))
    ]
    for copy in copies:
        copy.start()
    for part in range(4):
        for h in range(4 * part, 4 * part + 4):
            m[h] = mm(z[h], f[h]) * scale
        hs = pl.ds(4 * part, 4)
        copy = pltpu.make_async_copy(m.at[hs], m_out.at[hs], m_sem.at[part])
        copy.start()
        copies.append(copy)
    for copy in copies:
        copy.wait()


def per_device(queries, key_rows, values, out_grad, feature_map):
    tokens, width = queries.shape
    dma = pltpu.SemaphoreType.DMA
    state = (HD, HD)
    flat = jax.ShapeDtypeStruct((tokens, width), BF16)
    rows = (tokens, width)
    query_grad, key_grad, value_grad, z = pl.pallas_call(
        kernel,
        out_shape=(flat, flat, flat, jax.ShapeDtypeStruct((HEADS,) + state, BF16)),
        in_specs=[pl.BlockSpec(memory_space=pltpu.HBM)] * 5,
        out_specs=[pl.BlockSpec(memory_space=pl.ANY)] * 4,
        scratch_shapes=[
            pltpu.VMEM(rows, BF16), pltpu.VMEM(rows, BF16), pltpu.VMEM(rows, BF16), pltpu.VMEM(rows, BF16),
            pltpu.VMEM((HEADS,) + state, BF16),
            pltpu.VMEM(rows, BF16), pltpu.VMEM(rows, BF16), pltpu.VMEM(rows, BF16),
            pltpu.VMEM((NX, QUARTER, 2) + state, BF16),
            pltpu.VMEM((NX, QUARTER, 2) + state, BF16),
            pltpu.VMEM((NX, QUARTER) + state, BF16),
            pltpu.VMEM((NX, QUARTER) + state, BF16),
            pltpu.VMEM((QUARTER, 2) + state, BF16),
            pltpu.VMEM((NY, QUARTER, 2, SLICE, HD), BF16),
            pltpu.VMEM((NY, QUARTER, 2, SLICE, HD), BF16),
            pltpu.VMEM((QUARTER, 2) + state, BF16),
            pltpu.VMEM((QUARTER,) + state, F32),
            pltpu.VMEM((QUARTER,) + state, BF16),
            pltpu.VMEM((NY, QUARTER, SLICE, HD), BF16),
            pltpu.VMEM((QUARTER, SLICE, HD), BF16),
            pltpu.VMEM((QUARTER,) + state, BF16),
            pltpu.VMEM((HEADS,) + state, BF16),
            pltpu.VMEM((NX, QUARTER, 2) + state, BF16),
            pltpu.VMEM((HEADS, 2) + state, BF16),
            pltpu.VMEM((HEADS,) + state, BF16),
            pltpu.VMEM((HEADS,) + state, BF16),
            pltpu.VMEM((HEADS,) + state, F32), pltpu.VMEM((HEADS,) + state, F32), pltpu.VMEM((HEADS,) + state, F32),
            dma((5,)), dma((CHUNKS, NX, 3)), dma,
            *[dma((CHUNKS, NX - 1))] * 4,
            *[dma((CHUNKS, NY - 1))] * 4,
            *[dma((CHUNKS, NX - 1))] * 2,
            *[dma((CHUNKS, NY - 1))] * 4,
            *[dma((CHUNKS, NX - 1))] * 2,
        ],
        compiler_params=pltpu.CompilerParams(
            collective_id=0, has_side_effects=True, vmem_limit_bytes=48 * 1024 * 1024
        ),
    )(*(pltpu.with_memory_space_constraint(a, pltpu.HBM) for a in (queries, key_rows, values, out_grad, feature_map)))
    whole = pl.BlockSpec(memory_space=pltpu.VMEM)
    return pl.pallas_call(
        functools.partial(emit, scale=1.0 / math.sqrt(tokens * lax.axis_size("ctx"))),
        out_shape=(flat, flat, flat, jax.ShapeDtypeStruct((HEADS,) + state, F32)),
        in_specs=[pl.BlockSpec(memory_space=pl.ANY)] * 3 + [whole] * 2,
        out_specs=[pl.BlockSpec(memory_space=pl.ANY)] * 4,
        scratch_shapes=[pltpu.VMEM((HEADS,) + state, F32), dma((3,)), dma((4,))],
        compiler_params=pltpu.CompilerParams(vmem_limit_bytes=8 * 1024 * 1024),
    )(query_grad, key_grad, value_grad, z, feature_map)


def solution(mesh):
    placed = P(("seq", "ctx"), None)
    return jax.shard_map(
        per_device,
        mesh=mesh,
        in_specs=(placed, placed, placed, placed, P()),
        out_specs=(placed, placed, placed, P("seq", None, None)),
        check_vma=False,
    )
```

time: 68.6 us -> 50.1 us (0.73)
  Pallas kernels: 58.8 us -> 49.3 us
  local copies, waits for them, and re-layouts: 7.58 us -> 0.01 us
  matrix products: 1.26 us -> 0 us
    pallas_call x1, Pallas kernels: 58.8 us -> 47.7 us  [per_device(): pl.pallas_call(kernel, out_shape=(flat, flat, flat, jax.ShapeDtypeStruct(...]
    unnamed x13 -> x2, local copies, waits for them, and re-layouts: 7.58 us -> 0.01 us
    pallas_call x0 -> x1, Pallas kernels: none -> 1.54 us  [per_device(): pl.pallas_call(functools.partial(emit, scale=1.0 / math.sqrt(tokens * lax...]
    dot_general x1 -> x0, matrix products: 1.26 us -> none  [per_device(): jnp.einsum('hcd,hde->hce', z, feature_map, preferred_element_type=F32)]
where the time goes in v2:
time: 50.1 us; the launch traced here: 49.9 us
  Pallas kernels  49.3 us (98%)
  between operations  0.66 us (1%)
    pallas_call x1, Pallas kernels, per_device(): pl.pallas_call(kernel, out_shape=(flat, flat, flat, jax.ShapeDtypeStruct(...  47.7 us
    pallas_call x1, Pallas kernels, per_device(): pl.pallas_call(functools.partial(emit, scale=1.0 / math.sqrt(tokens * lax...  1.54 us

profile of v2, /device:TPU:448, one launch (start us, length us, event | category | flops | bytes accessed | tf_op | source)
XLA Modules:
  0.0 49.9 jit_solution(10274720545419599432)
XLA Ops:
  0.6 0.0 copy-start
  0.6 47.7 %shard_map.84 = (bf16[128,2048]{1,0:T(8,128)(2,1)S(1)}, bf16[128,2048]{1,0:T(8,128)(2,1)S(1)}, bf16[128,2048]{1,0:T(8,128)(2,1)S(1)}, bf16[16,128,128]{2,1,0:T(8,128)(2,1)S(1)}) custom-call(bf16[128,2048]{1,0:T(8,128)(2,1)} %q_in.1, bf16[128,2048]{1,0:T(8,128)(2,1)} %k_in.1, bf16[128,2048]{1,0:T(8,128)(2,1)} %v_in.1, bf16[128,2048]{1,0:T(8,128)(2,1)} %g_in.1, ...), custom_call_target="tpu_custom_call" | custom-call | tf_op jit(solution)/shard_map/pallas_call | solution.py:404
  48.4 0.0 copy-done
  48.4 1.5 %shard_map.85 = (bf16[128,2048]{1,0:T(8,128)(2,1)}, bf16[128,2048]{1,0:T(8,128)(2,1)}, bf16[128,2048]{1,0:T(8,128)(2,1)}, f32[16,128,128]{2,1,0:T(8,128)}) custom-call(bf16[128,2048]{1,0:T(8,128)(2,1)S(1)} %get-tuple-element.8.q_in, bf16[128,2048]{1,0:T(8,128)(2,1)S(1)} %get-tuple-element.9.k_in, bf16[128,2048]{1,0:T(8,128)(2,1)S(1)} %get-tuple-element.10.v_in, ...), custom_call_target="tpu_custom_call" | custom-call | tf_op jit(solution)/shard_map/pallas_call | solution.py:444
Async XLA Ops:
  0.6 47.8 %copy-start = (bf16[16,128,128]{2,1,0:T(8,128)(2,1)S(1)}, bf16[16,128,128]{2,1,0:T(8,128)(2,1)}, u32[]{:S(2)}) copy-start(bf16[16,128,128]{2,1,0:T(8,128)(2,1)} %f.1) | copy-start | bytes 1572868

commit v3 on v2

--- a/solution.py
+++ b/solution.py
@@ -17,6 +17,7 @@
 HEADS = 16
 QUARTER = HEADS // NX
 CHUNKS = 4
+COLUMN_FIRST = (0, 1, )
 PER = QUARTER // CHUNKS
 HD = 128
 SLICE = HD // NY
@@ -31,10 +32,10 @@
     q_out, k_out, v_out, z_out,
     q, k, v, g, f, dq, dk, dv,
     sent, got, y_sent, y_got, total, col, carry, carried,
-    w_row, z_row, col_z, z_part, z_full, z_all,
+    w_row, z_row, col_z, z_part, z_full, z_all, y_col, y_sum, y_part,
     out_send, fin, h_mat, kh, aq, ak, av,
     in_sem, out_sem, z_sem,
-    p1s, p1r, ys, yr, p2s, p2r, p3s, p3r, p4s, p4r, z2s, z2r, z3s, z3r, z4s, z4r,
+    p1s, p1r, ys, yr, p2s, p2r, p3s, p3r, p4s, p4r, z2s, z2r, z3s, z3r, z4s, z4r, ycs, ycr, yxs, yxr,
 ):
     me = lax.axis_index("ctx")
     y = me // NX
@@ -123,6 +124,14 @@
             return z_all.at[pl.ds(i * QUARTER + c * PER, PER)]
 
         return along_x(lambda i: hs(x), hs, z4s, z4r, c, d, into)
+
+    def y_down(c, d, into=False):
+        js = pl.ds(c * PER, PER)
+        return along_y(lambda i: y_sent.at[:, js, rows_of(i)], lambda i: y_col.at[i, :, js], ycs, ycr, c, d, into)
+
+    def y_over(c, d, into=False):
+        js = pl.ds(c * PER, PER)
+        return along_x(lambda i: y_sum.at[i, js], lambda i: y_part.at[i, js], yxs, yxr, c, d, into)
 
     x_order = (2, 1, 3)
     y_order = (4, 3, 5, 2, 6, 1, 7)
@@ -173,14 +182,34 @@
         xo = at_x(d)
         for j in heads_of(c):
             part = local(xo * QUARTER + j)
-            if d:
+            if d or c in COLUMN_FIRST:
                 y_sent[xo, j] = part
             else:
                 y_got[x, j] = part
 
     def send_y(c):
-        for d in x_order:
-            p_y(c, d).start()
+        if c in COLUMN_FIRST:
+            for d in y_order:
+                y_down(c, d).start()
+            for j in heads_of(c):
+                for i in range(NX):
+                    y_col[y, i, j] = y_sent[i, j, rows_of(y)]
+        else:
+            for d in x_order:
+                p_y(c, d).start()
+
+    def column_y(c):
+        for d in y_order:
+            y_down(c, d, True).wait_recv()
+        for j in heads_of(c):
+            for i in range(NX):
+                w = y_col[0, i, j].astype(F32)
+                for n in range(1, NY):
+                    w += y_col[n, i, j].astype(F32)
+                y_sum[i, j] = w.astype(BF16)
+            y_part[x, j] = y_sum[x, j]
+        for d in x_order:
+            y_over(c, d).start()
 
     def sums(j):
         ks = [got[i, j, 0].astype(F32) for i in range(NX)]
@@ -244,13 +273,15 @@
             w_row[j] = w
 
     def row_z(c):
-        for d in x_order:
-            p_y(c, d, True).wait_recv()
+        if c not in COLUMN_FIRST:
+            for d in x_order:
+                p_y(c, d, True).wait_recv()
         for j in heads_of(c):
             later = col[:, j, 1].reshape(HD, HD)
             w = w_row[j] + mm(later, carry[:, j, 0].reshape(HD, HD), 0, 0)
-            for i in range(NX):
-                w += y_got[i, j].astype(F32)
+            if c not in COLUMN_FIRST:
+                for i in range(NX):
+                    w += y_got[i, j].astype(F32)
             z_row[j] = w.astype(BF16)
             col_z[y, j] = z_row[j, rows_of(y)]
         for d in y_order:
@@ -259,10 +290,16 @@
     def col_z_sum(c):
         for d in y_order:
             z2(c, d, True).wait_recv()
+        if c in COLUMN_FIRST:
+            for d in x_order:
+                y_over(c, d, True).wait_recv()
         for j in heads_of(c):
             w = col_z[0, j].astype(F32)
             for i in range(1, NY):
                 w += col_z[i, j].astype(F32)
+            if c in COLUMN_FIRST:
+                for i in range(NX):
+                    w += y_part[i, j].astype(F32)
             z_part[j] = w.astype(BF16)
             z_full[j, rows_of(y)] = z_part[j]
         for d in y_order:
@@ -291,13 +328,14 @@
     outs = []
 
     def finish(c):
-        for n, d in enumerate((0, 1, 3, 2)):
-            if d:
-                p4(c, d, True).wait_recv()
-            xo = at_x(-d)
+        places = (0, 1, 3, 2)
+        for d in places[1:]:
+            p4(c, d, True).wait_recv()
+        for d in places:
             for j in heads_of(c):
-                finish_head(xo * QUARTER + j)
-            part = cols(xo * QUARTER + c * PER, PER)
+                finish_head(at_x(-d) * QUARTER + j)
+        for n, d in enumerate(places):
+            part = cols(at_x(-d) * QUARTER + c * PER, PER)
             for i, (a, b) in enumerate(((dq, q_out), (dk, k_out), (dv, v_out))):
                 copy = pltpu.make_async_copy(a.at[:, part], b.at[:, part], out_sem.at[c, n, i])
                 copy.start()
@@ -316,24 +354,27 @@
     loads[4].wait()
     block_span(0, 1)
     send_states(1)
-    block_span(1, 5)
+    block_span(1, 4)
+    send_y(0)
+    block_span(4, 5)
     send_states(2)
     row_sums(0)
     block_span(5, 8)
     send_states(3)
     row_sums(1)
+    send_y(1)
     block_span(8, 12)
     scan(0)
     row_sums(2)
-    send_y(0)
     block_span(12, 14)
-    send_y(1)
+    column_y(0)
     scan(1)
     row_sums(3)
     send_y(2)
     block_span(14, 16)
     send_y(3)
     row_back(0)
+    column_y(1)
     scan(2)
     row_w(0)
     row_z(0)
@@ -349,15 +390,15 @@
     col_z_sum(0)
     row_back(3)
     col_z_sum(1)
-    finish(0)
     col_z_sum(2)
     col_z_sum(3)
+    finish(0)
     row_z_back(0)
+    row_z_back(1)
     finish(1)
-    row_z_back(1)
-    finish(2)
     row_z_back(2)
     row_z_back(3)
+    finish(2)
     finish(3)
     for c in range(CHUNKS):
         for d in x_order:
@@ -366,11 +407,12 @@
     z_copy.start()
 
     for c in range(CHUNKS):
-        for d in x_order:
-            for p in (p1, p_y, p4, z4):
+        early = c in COLUMN_FIRST
+        for d in x_order:
+            for p in (p1, y_over if early else p_y, p4, z4):
                 p(c, d).wait_send()
         for d in y_order:
-            for p in (p2, p3, z2, z3):
+            for p in (p2, p3, z2, z3) + ((y_down,) if early else ()):
                 p(c, d).wait_send()
     for copy in outs:
         copy.wait()
@@ -424,6 +466,9 @@
             pltpu.VMEM((QUARTER, SLICE, HD), BF16),
             pltpu.VMEM((QUARTER,) + state, BF16),
             pltpu.VMEM((HEADS,) + state, BF16),
+            pltpu.VMEM((NY, NX, QUARTER, SLICE, HD), BF16),
+            pltpu.VMEM((NX, QUARTER, SLICE, HD), BF16),
+            pltpu.VMEM((NX, QUARTER, SLICE, HD), BF16),
             pltpu.VMEM((NX, QUARTER, 2) + state, BF16),
             pltpu.VMEM((HEADS, 2) + state, BF16),
             pltpu.VMEM((HEADS,) + state, BF16),
@@ -434,6 +479,8 @@
             *[dma((CHUNKS, NY - 1))] * 4,
             *[dma((CHUNKS, NX - 1))] * 2,
             *[dma((CHUNKS, NY - 1))] * 4,
+            *[dma((CHUNKS, NX - 1))] * 2,
+            *[dma((CHUNKS, NY - 1))] * 2,
             *[dma((CHUNKS, NX - 1))] * 2,
         ],
         compiler_params=pltpu.CompilerParams(

time: 50.1 us -> 51.5 us (1.028)
  Pallas kernels: 49.3 us -> 50.7 us
    pallas_call x1, Pallas kernels: 47.7 us -> 49.2 us  [per_device(): pl.pallas_call(kernel, out_shape=(flat, flat, flat, jax.ShapeDtypeStruct(...]
where the time goes in v3:
time: 51.5 us; the launch traced here: 51.4 us
  Pallas kernels  50.7 us (98%)
  between operations  0.66 us (1%)
    pallas_call x1, Pallas kernels, per_device(): pl.pallas_call(kernel, out_shape=(flat, flat, flat, jax.ShapeDtypeStruct(...  49.2 us
    pallas_call x1, Pallas kernels, per_device(): pl.pallas_call(functools.partial(emit, scale=1.0 / math.sqrt(tokens * lax...  1.54 us

profile of v3, /device:TPU:448, one launch (start us, length us, event | category | flops | bytes accessed | tf_op | source)
XLA Modules:
  0.0 51.4 jit_solution(15382784998262710413)
XLA Ops:
  0.6 0.0 copy-start
  0.6 49.2 %shard_map.84 = (bf16[128,2048]{1,0:T(8,128)(2,1)S(1)}, bf16[128,2048]{1,0:T(8,128)(2,1)S(1)}, bf16[128,2048]{1,0:T(8,128)(2,1)S(1)}, bf16[16,128,128]{2,1,0:T(8,128)(2,1)S(1)}) custom-call(bf16[128,2048]{1,0:T(8,128)(2,1)} %q_in.1, bf16[128,2048]{1,0:T(8,128)(2,1)} %k_in.1, bf16[128,2048]{1,0:T(8,128)(2,1)} %v_in.1, bf16[128,2048]{1,0:T(8,128)(2,1)} %g_in.1, ...), custom_call_target="tpu_custom_call" | custom-call | tf_op jit(solution)/shard_map/pallas_call | solution.py:446
  49.8 0.0 copy-done
  49.9 1.5 %shard_map.85 = (bf16[128,2048]{1,0:T(8,128)(2,1)}, bf16[128,2048]{1,0:T(8,128)(2,1)}, bf16[128,2048]{1,0:T(8,128)(2,1)}, f32[16,128,128]{2,1,0:T(8,128)}) custom-call(bf16[128,2048]{1,0:T(8,128)(2,1)S(1)} %get-tuple-element.8.q_in, bf16[128,2048]{1,0:T(8,128)(2,1)S(1)} %get-tuple-element.9.k_in, bf16[128,2048]{1,0:T(8,128)(2,1)S(1)} %get-tuple-element.10.v_in, ...), custom_call_target="tpu_custom_call" | custom-call | tf_op jit(solution)/shard_map/pallas_call | solution.py:491
Async XLA Ops:
  0.6 49.2 %copy-start = (bf16[16,128,128]{2,1,0:T(8,128)(2,1)S(1)}, bf16[16,128,128]{2,1,0:T(8,128)(2,1)}, u32[]{:S(2)}) copy-start(bf16[16,128,128]{2,1,0:T(8,128)(2,1)} %f.1) | copy-start | bytes 1572868

commit v4 on v2

--- a/solution.py
+++ b/solution.py
@@ -53,7 +53,7 @@
         pltpu.make_async_copy(a, b, in_sem.at[i])
         for i, (a, b) in enumerate(((k_in, k), (v_in, v), (q_in, q), (g_in, g), (f_in, f)))
     ]
-    for load in loads:
+    for load in loads[:4]:
         load.start()
 
     barrier = pltpu.get_barrier_semaphore()
@@ -63,6 +63,7 @@
         pl.semaphore_signal(barrier, inc=1, device_id=place(at_y(d), x), device_id_type=MESH)
     for load in loads[:4]:
         load.wait()
+    loads[4].start()
     pl.semaphore_wait(barrier, NX + NY - 2)
 
     def cols(h, n=1):
@@ -291,13 +292,14 @@
     outs = []
 
     def finish(c):
-        for n, d in enumerate((0, 1, 3, 2)):
-            if d:
-                p4(c, d, True).wait_recv()
-            xo = at_x(-d)
+        places = (0, 1, 3, 2)
+        for d in places[1:]:
+            p4(c, d, True).wait_recv()
+        for d in places:
             for j in heads_of(c):
-                finish_head(xo * QUARTER + j)
-            part = cols(xo * QUARTER + c * PER, PER)
+                finish_head(at_x(-d) * QUARTER + j)
+        for n, d in enumerate(places):
+            part = cols(at_x(-d) * QUARTER + c * PER, PER)
             for i, (a, b) in enumerate(((dq, q_out), (dk, k_out), (dv, v_out))):
                 copy = pltpu.make_async_copy(a.at[:, part], b.at[:, part], out_sem.at[c, n, i])
                 copy.start()
@@ -349,15 +351,15 @@
     col_z_sum(0)
     row_back(3)
     col_z_sum(1)
-    finish(0)
     col_z_sum(2)
     col_z_sum(3)
+    finish(0)
     row_z_back(0)
+    row_z_back(1)
     finish(1)
-    row_z_back(1)
-    finish(2)
     row_z_back(2)
     row_z_back(3)
+    finish(2)
     finish(3)
     for c in range(CHUNKS):
         for d in x_order:

time: 50.1 us -> 50.1 us (level)
  no operation moved by 1% of the time
where the time goes in v4:
time: 50.1 us; the launch traced here: 49.9 us
  Pallas kernels  49.3 us (98%)
  between operations  0.66 us (1%)
    pallas_call x1, Pallas kernels, per_device(): pl.pallas_call(kernel, out_shape=(flat, flat, flat, jax.ShapeDtypeStruct(...  47.7 us
    pallas_call x1, Pallas kernels, per_device(): pl.pallas_call(functools.partial(emit, scale=1.0 / math.sqrt(tokens * lax...  1.54 us

profile of v4, /device:TPU:448, one launch (start us, length us, event | category | flops | bytes accessed | tf_op | source)
XLA Modules:
  0.0 49.9 jit_solution(12120927700997940804)
XLA Ops:
  0.6 0.0 copy-start
  0.6 47.7 %shard_map.84 = (bf16[128,2048]{1,0:T(8,128)(2,1)S(1)}, bf16[128,2048]{1,0:T(8,128)(2,1)S(1)}, bf16[128,2048]{1,0:T(8,128)(2,1)S(1)}, bf16[16,128,128]{2,1,0:T(8,128)(2,1)S(1)}) custom-call(bf16[128,2048]{1,0:T(8,128)(2,1)} %q_in.1, bf16[128,2048]{1,0:T(8,128)(2,1)} %k_in.1, bf16[128,2048]{1,0:T(8,128)(2,1)} %v_in.1, bf16[128,2048]{1,0:T(8,128)(2,1)} %g_in.1, ...), custom_call_target="tpu_custom_call" | custom-call | tf_op jit(solution)/shard_map/pallas_call | solution.py:406
  48.4 0.0 copy-done
  48.4 1.5 %shard_map.85 = (bf16[128,2048]{1,0:T(8,128)(2,1)}, bf16[128,2048]{1,0:T(8,128)(2,1)}, bf16[128,2048]{1,0:T(8,128)(2,1)}, f32[16,128,128]{2,1,0:T(8,128)}) custom-call(bf16[128,2048]{1,0:T(8,128)(2,1)S(1)} %get-tuple-element.8.q_in, bf16[128,2048]{1,0:T(8,128)(2,1)S(1)} %get-tuple-element.9.k_in, bf16[128,2048]{1,0:T(8,128)(2,1)S(1)} %get-tuple-element.10.v_in, ...), custom_call_target="tpu_custom_call" | custom-call | tf_op jit(solution)/shard_map/pallas_call | solution.py:446
Async XLA Ops:
  0.6 47.8 %copy-start = (bf16[16,128,128]{2,1,0:T(8,128)(2,1)S(1)}, bf16[16,128,128]{2,1,0:T(8,128)(2,1)}, u32[]{:S(2)}) copy-start(bf16[16,128,128]{2,1,0:T(8,128)(2,1)} %f.1) | copy-start | bytes 1572868
